TPU v7x, 32 devices: a whole 2x2x4 slice. The times are simulated.
32 devices in a mesh: groups: 2 (over y), tensor: 4 (over z), store: 4 (over x, core).
Axes of the slice: x: 2, y: 2, z: 4, core: 2. Of those that a mesh axis runs over, the one named last changes fastest.
Arguments:
- tokens: bfloat16 [4096, 8192], P(('groups', 'store', 'tensor')), parts along dimension 0, may hold values from -32 to 32
- query_weight: bfloat16 [8192, 8192], P(None, 'tensor'), may hold values from -0.0625 to 0.0625
- key_value_weight: bfloat16 [8192, 2048], P(None, 'tensor'), may hold values from -0.0625 to 0.0625
- adapter_down_maps: bfloat16 [32, 128, 8192], P('store', None, 'tensor'), may hold values from -0.0625 to 0.0625
- adapter_up_query: bfloat16 [32, 64, 8192], P('store', None, 'tensor'), may hold values from -0.375 to 0.375
- adapter_up_key_value: bfloat16 [32, 64, 2048], P('store', None, 'tensor'), may hold values from -0.375 to 0.375
- adapter_row_table: int32 [64], P('groups'), parts along dimension 0, may hold values from 0 to 31, as said below
- request_adapter_ids: int32 [8, 4], P('groups'), parts along dimension 0, may hold values from 0 to 31, as said below
- token_request_ids: int32 [8, 512], P(('groups', 'store')), parts along dimension 0, may hold values from 0 to 3, never falling along the last dimension, each value on 1 to 256 neighbouring positions
Outputs:
- attention: bfloat16 [4096, 8192], P(('groups', 'store'), 'tensor'), parts along dimension 0
There are 2 independent parts, one for each index of `groups`. A program takes and returns all parts, laid end to end along the dimension named above; an argument that names none is the same for every part. Nothing has to cross between parts.
Inputs may be any that keep to these rules, and one draw needn't show every extreme that they name: A permutation: adapter a lies in row adapter_row_table[a] of the adapter arrays, on store index adapter_row_table[a] // 8. `request_adapter_ids`: the 4 requests of one store batch use adapters held on 4 different store indices. `token_request_ids`: requests are contiguous runs of a store batch, each of 1 to 256 tokens.
All inputs are finite; a program needn't handle non-finite values.
Results may differ from a plain program's by a relative error of at most 0.012.
The roundings to bfloat16 on the way count: a program that leaves them out, or rounds other values in their place, can miss the bound.
Values may be sent and summed in bfloat16 or wider, within the bound.
A program may use at most 128 MiB of HBM per device.

v0:
```python
import math

import jax
import jax.numpy as jnp
from jax import lax
from jax.sharding import PartitionSpec as P

MODEL_WIDTH = 8192
QUERY_HEADS = 64
KEY_VALUE_HEADS = 8
HEAD_SIZE = 128
ADAPTER_RANK = 64
STORE_REQUESTS = 4
TOK_ST = 512


adapter_scale = 2.0
rope_theta = 500000.0


def from_partner(shard, axis, bit):
    return lax.ppermute(shard, axis, [(i, i ^ 1 << bit) for i in range(lax.axis_size(axis))])


def token_positions(segment_row):
    members = segment_row[:, None] == jnp.arange(STORE_REQUESTS, dtype=jnp.int32)[None, :]
    counts = jnp.sum(members.astype(jnp.int32), axis=0)
    starts = jnp.cumsum(counts) - counts
    first_index = jnp.sum(jnp.where(members, starts[None, :], 0), axis=1)
    return jnp.arange(segment_row.shape[0], dtype=jnp.int32) - first_index


def rotary(heads_values, positions):
    half_size = heads_values.shape[-1] // 2
    exponent = jnp.arange(half_size, dtype=jnp.float32) * (2.0 / heads_values.shape[-1])
    frequency = jnp.exp(-exponent * math.log(rope_theta))
    angles = positions.astype(jnp.float32)[:, None] * frequency[None, :]
    cosine = jnp.cos(angles)[:, None, :]
    sine = jnp.sin(angles)[:, None, :]
    lower = heads_values[..., :half_size]
    upper = heads_values[..., half_size:]
    return jnp.concatenate([lower * cosine - upper * sine, upper * cosine + lower * sine], axis=-1)


def select_rows(selector, stack):
    flat = stack.reshape(stack.shape[0], -1)
    picked = jnp.dot(selector, flat, preferred_element_type=jnp.float32)
    return picked.reshape(selector.shape[:-1] + stack.shape[1:])


def on_device(
    tokens,
    query_weight,
    key_value_weight,
    adapter_down_maps,
    adapter_up_query,
    adapter_up_key_value,
    adapter_row_table,
    request_adapter_ids,
    token_request_ids,
):
    tensor_rank = lax.axis_index("tensor")
    store_rank = lax.axis_index("store")
    tensor_count = lax.axis_size("tensor")
    store_count = lax.axis_size("store")
    position_count = adapter_down_maps.shape[0]
    adapter_total = adapter_row_table.shape[0]
    lookup = (
        request_adapter_ids[:, :, None] == jnp.arange(adapter_total, dtype=jnp.int32)[None, None, :]
    ).astype(jnp.int32)
    slot_table = jnp.sum(lookup * adapter_row_table[None, None, :], axis=2)
    my_slots = lax.dynamic_index_in_dim(slot_table, store_rank, 0, keepdims=False)
    local_slots = store_rank * position_count + jnp.arange(position_count, dtype=jnp.int32)
    serving = jnp.sum(
        (slot_table[:, :, None] == local_slots[None, None, :]).astype(jnp.int32), axis=1
    ).astype(jnp.bfloat16)
    out_down = select_rows(serving, adapter_down_maps).astype(jnp.bfloat16)
    out_query = select_rows(serving, adapter_up_query).astype(jnp.bfloat16)
    out_keyval = select_rows(serving, adapter_up_key_value).astype(jnp.bfloat16)
    got_down, got_query, got_keyval = (
        lax.all_to_all(out_down, "store", split_axis=0, concat_axis=0, tiled=True),
        lax.all_to_all(out_query, "store", split_axis=0, concat_axis=0, tiled=True),
        lax.all_to_all(out_keyval, "store", split_axis=0, concat_axis=0, tiled=True),
    )
    holder_pick = (
        (my_slots // position_count)[:, None] == jnp.arange(store_count, dtype=jnp.int32)[None, :]
    ).astype(jnp.bfloat16)
    down_blocks = select_rows(holder_pick, got_down).astype(jnp.bfloat16)
    up_query_blocks = select_rows(holder_pick, got_query).astype(jnp.bfloat16)
    up_keyval_blocks = select_rows(holder_pick, got_keyval).astype(jnp.bfloat16)
    segment_row = token_request_ids[0]
    members = segment_row[:, None] == jnp.arange(STORE_REQUESTS, dtype=jnp.int32)[None, :]
    member_float = members.astype(jnp.float32)
    member_half = members.astype(jnp.bfloat16)
    width_share = MODEL_WIDTH // tensor_count
    column_first = tensor_rank * width_share
    down_matrix = down_blocks.reshape(STORE_REQUESTS * 2 * ADAPTER_RANK, width_share)
    query_width = query_weight.shape[1]
    keyval_width = key_value_weight.shape[1]
    rows_piece = lax.all_gather(tokens, "tensor", axis=0, tiled=True)
    count = rows_piece.shape[0]
    plain_query = jnp.dot(rows_piece, query_weight, preferred_element_type=jnp.float32)
    plain_key_value = jnp.dot(rows_piece, key_value_weight, preferred_element_type=jnp.float32)
    features = lax.dynamic_slice_in_dim(rows_piece, column_first, width_share, 1)
    partial_low = lax.dot_general(
        features, down_matrix, (((1,), (1,)), ((), ())), preferred_element_type=jnp.float32
    )
    partial_low = jnp.sum(
        partial_low.reshape(count, STORE_REQUESTS, 2 * ADAPTER_RANK) * member_float[:, :, None],
        axis=1,
    )
    joined = jnp.concatenate([plain_query, plain_key_value, partial_low], axis=1)
    plain_query = joined[:, :query_width]
    plain_key_value = joined[:, query_width : query_width + keyval_width]
    low = lax.psum(joined[:, query_width + keyval_width :], "tensor").astype(jnp.bfloat16)
    token_query_update = (low[:, None, :ADAPTER_RANK] * member_half[:, :, None]).reshape(
        TOK_ST, STORE_REQUESTS * ADAPTER_RANK
    )
    token_key_value_update = (low[:, None, ADAPTER_RANK:] * member_half[:, :, None]).reshape(
        TOK_ST, STORE_REQUESTS * ADAPTER_RANK
    )
    query_update = jnp.dot(
        token_query_update,
        up_query_blocks.reshape(STORE_REQUESTS * ADAPTER_RANK, query_width),
        preferred_element_type=jnp.float32,
    )
    key_value_update = jnp.dot(
        token_key_value_update,
        up_keyval_blocks.reshape(STORE_REQUESTS * ADAPTER_RANK, keyval_width),
        preferred_element_type=jnp.float32,
    )
    query_unrotated = plain_query + adapter_scale * query_update
    key_value_unrotated = plain_key_value + adapter_scale * key_value_update
    positions = token_positions(segment_row)
    head_local = query_width // HEAD_SIZE
    query = rotary(query_unrotated.reshape(TOK_ST, head_local, HEAD_SIZE), positions).astype(
        jnp.bfloat16
    )
    pair_heads = keyval_width // HEAD_SIZE
    keyval_heads = key_value_unrotated.reshape(TOK_ST, pair_heads, HEAD_SIZE)
    holds_keys = tensor_rank % 2 == 0
    own_part = jnp.where(holds_keys, rotary(keyval_heads, positions), keyval_heads).astype(
        jnp.bfloat16
    )
    other_part = from_partner(own_part, "tensor", 0)
    keys = jnp.where(holds_keys, own_part, other_part)
    values = jnp.where(holds_keys, other_part, own_part)
    group_size = QUERY_HEADS // KEY_VALUE_HEADS
    kv_used = max(head_local // group_size, 1)
    per_kv = head_local // kv_used
    kv_first = tensor_rank * head_local // group_size - tensor_rank // 2 * pair_heads
    keys_used = lax.dynamic_slice_in_dim(keys, kv_first, kv_used, 1)
    values_used = lax.dynamic_slice_in_dim(values, kv_first, kv_used, 1)
    grouped = query.reshape(TOK_ST, kv_used, per_kv, HEAD_SIZE)
    scores = jnp.einsum(
        "tkgd,skd->kgts", grouped, keys_used, preferred_element_type=jnp.float32
    ) / math.sqrt(HEAD_SIZE)
    token_index = jnp.arange(TOK_ST, dtype=jnp.int32)
    allowed = (segment_row[:, None] == segment_row[None, :]) & (
        token_index[:, None] >= token_index[None, :]
    )
    scores = jnp.where(allowed, scores, -1e30)
    scores = scores - jnp.max(scores, axis=-1, keepdims=True)
    weights = jnp.exp(scores)
    weights = (weights / jnp.sum(weights, axis=-1, keepdims=True)).astype(jnp.bfloat16)
    mixed = jnp.einsum("kgts,skd->tkgd", weights, values_used, preferred_element_type=jnp.float32)
    return mixed.reshape(TOK_ST, query_width).astype(jnp.bfloat16)


def solution(mesh):
    return jax.shard_map(
        on_device,
        mesh=mesh,
        in_specs=(
            P(("groups", "store", "tensor"), None),
            P(None, "tensor"),
            P(None, "tensor"),
            P("store", None, "tensor"),
            P("store", None, "tensor"),
            P("store", None, "tensor"),
            P("groups"),
            P("groups", None),
            P(("groups", "store"), None),
        ),
        out_specs=P(("groups", "store"), "tensor"),
        check_vma=False,
    )
```

profile of v0, /device:TPU:0, one launch (start us, length us, event | category | flops | bytes accessed | tf_op | source)
XLA Modules:
  0.0 270.4 jit_solution(15919129932199313101)
XLA Ops:
  8.3 1.4 convolution_convert_fusion.4
  10.5 4.2 %all-to-all-start.1 = ((bf16[4,64,512]{2,1,0:T(8,128)(2,1)}), bf16[4,64,512]{2,1,0:T(8,128)(2,1)S(1)}, u32[]{:S(2)}, u32[]{:S(2)}) async-start(bf16[4,64,512]{2,1,0:T(8,128)(2,1)} %copy.34), calls=%async_computation.1 | async-start | bytes 524288 | tf_op jit(solution)/shard_map/all_to_all | solution.py:83
  14.7 1.6 convolution_convert_fusion.3
  16.3 1.6 copy.40
  18.0 2.8 %all-to-all-done.1 = bf16[4,64,512]{2,1,0:T(8,128)(2,1)S(1)} async-done(((bf16[4,64,512]{2,1,0:T(8,128)(2,1)}), bf16[4,64,512]{2,1,0:T(8,128)(2,1)S(1)}, u32[]{:S(2)}, u32[]{:S(2)}) %all-to-all-start.1) | async-done | bytes 262176 | tf_op jit(solution)/shard_map/all_to_all | solution.py:83
  20.7 3.5 %all-to-all-start.2 = ((bf16[4,64,2048]{2,1,0:T(8,128)(2,1)}), bf16[4,64,2048]{2,1,0:T(8,128)(2,1)S(1)}, u32[]{:S(2)}, u32[]{:S(2)}) async-start(bf16[4,64,2048]{2,1,0:T(8,128)(2,1)} %copy.40), calls=%async_computation.2 | async-start | bytes 2097152 | tf_op jit(solution)/shard_map/all_to_all | solution.py:82
  24.6 5.4 %convolution_convert_fusion = bf16[4,128,2048]{2,0,1:T(4,128)(2,1)S(1)} fusion(s32[4,8]{1,0:T(4,128)S(1)} %convert_reduce_fusion.1, bf16[1,8,128,2048]{3,2,1,0:T(8,128)(2,1)} %bitcast.125), kind=kOutput, calls=%fused_computation.14 | convolution fusion | flops 17825824 | bytes 6291584 | tf_op jit(solution)/shard_map/dot_general | solution.py:47
  30.0 2.5 copy.31
  32.5 6.2 %all-to-all-done.2 = bf16[4,64,2048]{2,1,0:T(8,128)(2,1)S(1)} async-done(((bf16[4,64,2048]{2,1,0:T(8,128)(2,1)}), bf16[4,64,2048]{2,1,0:T(8,128)(2,1)S(1)}, u32[]{:S(2)}, u32[]{:S(2)}) %all-to-all-start.2) | async-done | bytes 1048608 | tf_op jit(solution)/shard_map/all_to_all | solution.py:82
  39.7 3.8 %all-to-all-start = ((bf16[4,128,2048]{2,1,0:T(8,128)(2,1)}), bf16[4,128,2048]{2,1,0:T(8,128)(2,1)S(1)}, u32[]{:S(2)}, u32[]{:S(2)}) async-start(bf16[4,128,2048]{2,1,0:T(8,128)(2,1)} %copy.31), calls=%async_computation | async-start | bytes 4194304 | tf_op jit(solution)/shard_map/all_to_all | solution.py:81
  45.2 3.3 %convolution_convert_fusion.2 = bf16[4,64,2048]{2,0,1:T(4,128)(2,1)} fusion(s32[4]{0:T(128)S(1)} %and_select_fusion, bf16[1,4,64,2048]{3,2,1,0:T(8,128)(2,1)} %bitcast.129), kind=kOutput, calls=%fused_computation.16 | convolution fusion | flops 4718608 | bytes 2097168 | tf_op jit(solution)/shard_map/dot_general | solution.py:47
  48.4 20.5 %all-to-all-done = bf16[4,128,2048]{2,1,0:T(8,128)(2,1)S(1)} async-done(((bf16[4,128,2048]{2,1,0:T(8,128)(2,1)}), bf16[4,128,2048]{2,1,0:T(8,128)(2,1)S(1)}, u32[]{:S(2)}, u32[]{:S(2)}) %all-to-all-start) | async-done | bytes 2097184 | tf_op jit(solution)/shard_map/all_to_all | solution.py:81
  68.9 3.1 %convolution_convert_fusion.1 = bf16[4,128,2048]{2,0,1:T(4,128)(2,1)} fusion(s32[4]{0:T(128)S(1)} %and_select_fusion, bf16[1,4,128,2048]{3,2,1,0:T(8,128)(2,1)S(1)} %bitcast.127), kind=kOutput, calls=%fused_computation.15 | convolution fusion | flops 9437200 | bytes 4194320 | tf_op jit(solution)/shard_map/dot_general | solution.py:47
  72.0 89.3 %all-gather.2.cloned.1.call-done = bf16[512,8192]{1,0:T(8,128)(2,1)} async-done(((bf16[128,8192]{1,0:T(8,128)(2,1)}), bf16[512,8192]{1,0:T(8,128)(2,1)}) %all-gather.2.cloned.1.call-update) | async-done | bytes 8388624 | tf_op jit(solution)/shard_map/all_gather | solution.py:100
  161.3 4.9 %fusion.24 = f32[512,128]{1,0:T(8,128)S(1)} fusion(bf16[4,128,2048]{2,0,1:T(4,128)(2,1)} %convolution_convert_fusion.1, bf16[512,8192]{1,0:T(8,128)(2,1)} %all-gather.2.cloned.1.call-done, s32[]{:T(128)S(6)} %select_n.62, f32[512,4]{0,1:T(4,128)S(1)} %get-tuple-element.14), kind=kOutput, calls=%fused_computation.31 | convolution fusion | flops 1074200576 | bytes 4464644 | tf_op jit(solution)/shard_map/dot_general | solution.py:105
  166.2 21.4 %all-reduce.1 = bf16[512,128]{1,0:T(8,128)(2,1)S(1)} all-reduce(f32[512,128]{1,0:T(8,128)S(1)} %fusion.24), channel_id=1, replica_groups=mesh['groups'=2,'tensor'=4,'store'=4] {'tensor'}, use_global_device_ids=true, to_apply=%region_3.4 | all-reduce | flops 65536 | bytes 393216 | tf_op jit(solution)/shard_map/psum | solution.py:115
  187.8 9.5 %fusion.82 = f32[512,512]{0,1:T(8,128)S(1)} fusion(bf16[512,8192]{1,0:T(8,128)(2,1)} %all-gather.2.cloned.1.call-done, bf16[8192,512]{1,0:T(8,128)(2,1)} %param.11), kind=kOutput, calls=%fused_computation.106 | convolution fusion | flops 4294967296 | bytes 17825792 | tf_op jit(solution)/shard_map/dot_general | solution.py:103
  198.9 23.8 %fusion.83 = f32[512,2048]{1,0:T(8,128)S(1)} fusion(bf16[512,8192]{1,0:T(8,128)(2,1)} %all-gather.2.cloned.1.call-done, bf16[8192,2048]{1,0:T(8,128)(2,1)} %param.10), kind=kOutput, calls=%fused_computation.107 | convolution fusion | flops 17179869184 | bytes 46137344 | tf_op jit(solution)/shard_map/dot_general | solution.py:102
  222.8 1.7 fusion.7
  225.5 1.8 subtract_convert_fusion
  228.4 8.2 %fusion.8 = f32[2,512,512,8]{2,1,3,0:T(8,128)} fusion(bf16[512,2,8,64]{3,0,2,1:T(8,128)(2,1)S(1)} %bitcast.123, bf16[512,2,8,64]{3,0,2,1:T(8,128)(2,1)S(1)} %bitcast.122, pred[]{:T(512)S(6)} %eq.43, bf16[512,4,128]{2,0,1:T(8,128)(2,1)S(1)} %fusion.29, s32[]{:T(128)S(6)} %select_n.70, bf16[512,4,128]{2,0,1:T(8,128)(2,1)S(1)} %collective-permute-done), kind=kOutput, calls=%fused_computation.18 | convolution fusion | flops 1078067200 | bytes 21495812 | tf_op jit(solution)/shard_map/tkgd,skd->kgts/dot_general | solution.py:155
  236.6 17.2 %fusion.69 = (f32[2,8,512]{2,1,0:T(8,128)S(1)}, f32[2,8,512,512]{2,3,1,0:T(8,128)}) fusion(f32[2,512,512,8]{2,1,3,0:T(8,128)} %fusion.8, pred[512,512]{0,1:T(8,128)(4,1)S(1)} %fusion.31), kind=kOutput, calls=%fused_computation.93 | output fusion | flops 25166336 | bytes 33849344 | tf_op jit(solution)/shard_map/sub | solution.py:163
  253.8 7.3 %fusion.16 = bf16[2,128,8,512]{3,1,2,0:T(8,128)(2,1)S(1)} fusion(f32[2,8,512,512]{2,3,1,0:T(8,128)} %get-tuple-element.16, f32[2,8,512]{2,1,0:T(8,128)S(1)} %get-tuple-element.15, pred[]{:T(512)S(6)} %eq.43, bf16[512,4,128]{2,0,1:T(8,128)(2,1)S(1)} %fusion.29, s32[]{:T(128)S(6)} %select_n.70, bf16[512,4,128]{2,0,1:T(8,128)(2,1)} %copy-done.3), kind=kOutput, calls=%fused_computation.26 | convolution fusion | flops 1083310080 | bytes 19431428 | tf_op jit(solution)/shard_map/kgts,skd->tkgd/dot_general | solution.py:166
  261.2 2.4 copy.46
  (39 shorter events, 9.2 us)
Async XLA Ops:
  6.5 8.2 %copy-start = (bf16[8,64,2048]{2,1,0:T(8,128)(2,1)S(1)}, bf16[8,64,2048]{2,1,0:T(8,128)(2,1)}, u32[]{:S(2)}) copy-start(bf16[8,64,2048]{2,1,0:T(8,128)(2,1)} %param.13) | copy-start | bytes 6291460
  6.5 154.7 %all-gather.2.cloned.1.call-start = ((), (), s32[]{:S(2)}) async-start(), calls=%async_computation.3 | async-start | bytes 10485760 | tf_op jit(solution)/shard_map/all_gather | solution.py:100
  9.7 14.6 %copy-start.4 = (s32[1,512]{1,0:T(1,128)S(1)}, s32[1,512]{1,0:T(1,128)}, u32[]{:S(2)}) copy-start(s32[1,512]{1,0:T(1,128)} %param.17) | copy-start | bytes 6148
  10.5 10.2 %all-to-all-start.1 = ((bf16[4,64,512]{2,1,0:T(8,128)(2,1)}), bf16[4,64,512]{2,1,0:T(8,128)(2,1)S(1)}, u32[]{:S(2)}, u32[]{:S(2)}) async-start(bf16[4,64,512]{2,1,0:T(8,128)(2,1)} %copy.34), calls=%async_computation.1 | async-start | bytes 524288 | tf_op jit(solution)/shard_map/all_to_all | solution.py:83
  20.7 17.9 %all-to-all-start.2 = ((bf16[4,64,2048]{2,1,0:T(8,128)(2,1)}), bf16[4,64,2048]{2,1,0:T(8,128)(2,1)S(1)}, u32[]{:S(2)}, u32[]{:S(2)}) async-start(bf16[4,64,2048]{2,1,0:T(8,128)(2,1)} %copy.40), calls=%async_computation.2 | async-start | bytes 2097152 | tf_op jit(solution)/shard_map/all_to_all | solution.py:82
  38.7 1.0 copy-start.2
  39.7 29.3 %all-to-all-start = ((bf16[4,128,2048]{2,1,0:T(8,128)(2,1)}), bf16[4,128,2048]{2,1,0:T(8,128)(2,1)S(1)}, u32[]{:S(2)}, u32[]{:S(2)}) async-start(bf16[4,128,2048]{2,1,0:T(8,128)(2,1)} %copy.31), calls=%async_computation | async-start | bytes 4194304 | tf_op jit(solution)/shard_map/all_to_all | solution.py:81
  198.8 23.9 %copy-start.1 = (bf16[4,64,2048]{2,0,1:T(4,128)(2,1)S(1)}, bf16[4,64,2048]{2,0,1:T(4,128)(2,1)}, u32[]{:S(2)}) copy-start(bf16[4,64,2048]{2,0,1:T(4,128)(2,1)} %convolution_convert_fusion.2) | copy-start | bytes 3145732
  198.8 29.6 %collective-permute-start = (bf16[512,4,128]{2,0,1:T(8,128)(2,1)S(1)}, bf16[512,4,128]{2,0,1:T(8,128)(2,1)S(1)}, u32[]{:S(2)}, u32[]{:S(2)}) collective-permute-start(bf16[512,4,128]{2,0,1:T(8,128)(2,1)S(1)} %fusion.29), channel_id=1, source_target_pairs={{0,4},{4,0},{8,12},{12,8},{1,5},{5,1},{9,13},{13,9},{2,6},{6,2},{1... | collective-permute-start | bytes 1572872 | tf_op jit(solution)/shard_map/ppermute | solution.py:22
  228.4 8.2 %copy-start.3 = (bf16[512,4,128]{2,0,1:T(8,128)(2,1)}, bf16[512,4,128]{2,0,1:T(8,128)(2,1)S(1)}, u32[]{:S(2)}) copy-start(bf16[512,4,128]{2,0,1:T(8,128)(2,1)S(1)} %collective-permute-done) | copy-start | bytes 1572868
Sparse Core Ops, SparseCore 0:
  8.9 152.3 all-gather.1
where the time goes:
time: 271 us; the launch traced here: 270 us
  waiting for transfers between devices  119 us (44%)
  matrix products  71 us (26%)
  other arithmetic  22.4 us (8%)
  blocking collectives  21.4 us (8%)
  between operations  13.7 us (5%)
  starting transfers between devices  11.6 us (4%)
  local copies, waits for them, and re-layouts  10.9 us (4%)
    all_gather x1, waiting for transfers between devices, on_device(): rows_piece = lax.all_gather(tokens, 'tensor', axis=0, tiled=True)  89.3 us
    dot_general x1, matrix products, on_device(): jnp.dot(rows_piece, query_weight, preferred_element_type=jnp.float32)  23.8 us
    psum x1, blocking collectives, on_device(): lax.psum(joined[:, query_width + keyval_width:], 'tensor')  21.4 us
    all_to_all x1, waiting for transfers between devices, on_device(): lax.all_to_all(out_down, 'store', split_axis=0, concat_axis=0, tiled=True)  20.5 us
    sub x1, other arithmetic, on_device(): scores = scores - jnp.max(scores, axis=-1, keepdims=True)  17.2 us
    dot_general x6, matrix products, select_rows(): picked = jnp.dot(selector, flat, preferred_element_type=jnp.float32)  15.1 us
    dot_general x1, matrix products, on_device(): jnp.dot(rows_piece, key_value_weight, preferred_element_type=jnp.float32)  9.46 us
    dot_general x1, matrix products, on_device(): jnp.einsum('tkgd,skd->kgts', grouped, keys_used, preferred_element_type=j...  8.15 us
  transfers between devices with their start and end apart: 5, of which 4 were waited for; matrix products, arithmetic and copies ran while one was open for 19% of the time, Pallas kernels for 0%

commit v1 on v0

v1 whole, which is shorter than its diff:
```python
import functools
import math

import jax
import jax.numpy as jnp
from jax import lax
from jax.experimental import pallas as pl
from jax.experimental.pallas import tpu as pltpu
from jax.sharding import PartitionSpec as P

MODEL_WIDTH = 8192
QUERY_HEADS = 64
KEY_VALUE_HEADS = 8
HEAD_SIZE = 128
ADAPTER_RANK = 64
STORE_REQUESTS = 4
TOK_ST = 512


adapter_scale = 2.0
rope_theta = 500000.0


def token_positions(segment_row):
    members = segment_row[:, None] == jnp.arange(STORE_REQUESTS, dtype=jnp.int32)[None, :]
    counts = jnp.sum(members.astype(jnp.int32), axis=0)
    starts = jnp.cumsum(counts) - counts
    first_index = jnp.sum(jnp.where(members, starts[None, :], 0), axis=1)
    return jnp.arange(segment_row.shape[0], dtype=jnp.int32) - first_index


MAX_RUN = 256
MESH = pl.DeviceIdType.MESH


def rotary_tables(positions):
    half_size = HEAD_SIZE // 2
    exponent = jnp.arange(half_size, dtype=jnp.float32) * (2.0 / HEAD_SIZE)
    frequency = jnp.exp(-exponent * math.log(rope_theta))
    angles = positions.astype(jnp.float32)[:, None] * frequency[None, :]
    cosine = jnp.cos(angles)
    sine = jnp.sin(angles)
    return (
        jnp.concatenate([cosine, cosine], axis=1),
        jnp.concatenate([-sine, sine], axis=1),
    )


def select_kernel(index_ref, down_ref, query_ref, keyval_ref, down_out, query_out, keyval_out):
    down_out[...] = down_ref[...]
    query_out[...] = query_ref[...]
    keyval_out[...] = keyval_ref[...]


def select_adapters(index, stacks):
    specs_in = [
        pl.BlockSpec((1,) + stack.shape[1:], lambda i, index_ref: (index_ref[i], 0, 0))
        for stack in stacks
    ]
    specs_out = [
        pl.BlockSpec((1,) + stack.shape[1:], lambda i, index_ref: (i, 0, 0)) for stack in stacks
    ]
    return pl.pallas_call(
        select_kernel,
        grid_spec=pltpu.PrefetchScalarGridSpec(
            num_scalar_prefetch=1,
            grid=(index.shape[0],),
            in_specs=specs_in,
            out_specs=specs_out,
        ),
        out_shape=[
            jax.ShapeDtypeStruct((index.shape[0],) + stack.shape[1:], stack.dtype)
            for stack in stacks
        ],
        name="select_adapters",
    )(index, *stacks)


def project_kernel(
    n,
    stores,
    chunks,
    tokens_ref,
    wq_hbm,
    wkv_hbm,
    down_hbm,
    upq_hbm,
    upkv_hbm,
    mask_ref,
    cos_ref,
    sin_ref,
    kcos_ref,
    ksin_ref,
    query_out,
    own_out,
    other_out,
    xbuf,
    wq,
    wkv,
    acc_q,
    acc_kv,
    down,
    upq,
    upkv,
    low_part,
    low_got,
    low_all,
    kv_heads,
    kv_got,
    token_sem,
    weight_sem,
    recv_sem,
    send_sem,
    adapter_send,
    adapter_recv,
    adapter_own,
    part_send,
    part_recv,
    low_send,
    low_recv,
    kv_sem,
):
    t = lax.axis_index("tensor")
    s = lax.axis_index("store")
    rows = tokens_ref.shape[0]
    width = tokens_ref.shape[1] // chunks
    total = rows * n
    query_width = wq.shape[1]
    keyval_width = wkv.shape[1]
    pair_heads = keyval_width // HEAD_SIZE
    head_local = query_width // HEAD_SIZE
    group_size = QUERY_HEADS // KEY_VALUE_HEADS
    kv_used = max(head_local // group_size, 1)

    def kv_first(rank):
        return rank * head_local // group_size - rank // 2 * pair_heads

    barrier = pltpu.get_barrier_semaphore()
    for d in range(1, n):
        pl.semaphore_signal(
            barrier, inc=1, device_id={"tensor": lax.rem(t + d, n)}, device_id_type=MESH
        )
    for d in range(1, stores):
        pl.semaphore_signal(
            barrier, inc=1, device_id={"store": lax.rem(s + d, stores)}, device_id_type=MESH
        )

    def own_copy(c):
        return pltpu.make_async_copy(
            tokens_ref.at[:, pl.ds(c * width, width)],
            xbuf.at[c, pl.ds(t * rows, rows), :],
            token_sem.at[c],
        )

    def weight_copies(c):
        part = pl.ds(c * width, width)
        return (
            pltpu.make_async_copy(wq_hbm.at[part, :], wq.at[part, :], weight_sem.at[0, c]),
            pltpu.make_async_copy(wkv_hbm.at[part, :], wkv.at[part, :], weight_sem.at[1, c]),
        )

    for c in range(chunks):
        own_copy(c).start()
        for copy in weight_copies(c):
            copy.start()
    adapter_pairs = ((down_hbm, down), (upq_hbm, upq), (upkv_hbm, upkv))

    def adapter_block(held, i, at):
        if i == 0:
            return held.at[at]
        return held.at[pl.ds(at * ADAPTER_RANK, ADAPTER_RANK), :]

    own_adapters = [
        pltpu.make_async_copy(source.at[s], adapter_block(held, i, s), adapter_own.at[i])
        for i, (source, held) in enumerate(adapter_pairs)
    ]
    for copy in own_adapters:
        copy.start()

    pl.semaphore_wait(barrier, n - 1 + stores - 1)

    def place(side, i):
        return chunks - 1 - i if side == 0 else i

    def stream_copy(side, p, i, own):
        c = place(side, i)
        shard = t - p if side == 0 else t + p
        held = xbuf.at[c, pl.ds(shard * rows, rows), :]
        source = tokens_ref.at[:, pl.ds(c * width, width)] if own else held
        return pltpu.make_async_remote_copy(
            src_ref=source,
            dst_ref=held,
            send_sem=send_sem.at[side, p, i],
            recv_sem=recv_sem.at[side, p, i],
            device_id={"tensor": t + 1 if side == 0 else t - 1},
            device_id_type=MESH,
        )

    def arrival(side, p, i):
        c = place(side, i)
        shard = t - p if side == 0 else t + p
        held = xbuf.at[c, pl.ds(shard * rows, rows), :]
        return pltpu.make_async_remote_copy(
            src_ref=held,
            dst_ref=held,
            send_sem=send_sem.at[side, p - 1, i],
            recv_sem=recv_sem.at[side, p - 1, i],
            device_id={"tensor": t - 1 if side == 0 else t + 1},
            device_id_type=MESH,
        )

    can_send = (t < n - 1, t > 0)
    for i in range(chunks):
        for side in range(2):

            @pl.when(can_send[side])
            def _():
                stream_copy(side, 0, i, True).start()

    adapter_sends = []
    for d in range(1, stores):
        for i, (source, held) in enumerate(adapter_pairs):
            peer = lax.rem(s + d, stores)
            copy = pltpu.make_async_remote_copy(
                src_ref=source.at[peer],
                dst_ref=adapter_block(held, i, s),
                send_sem=adapter_send.at[i, d],
                recv_sem=adapter_recv.at[i, d],
                device_id={"store": peer},
                device_id_type=MESH,
            )
            copy.start()
            adapter_sends.append(copy)

    tile_q = min(query_width, 512)

    def unit(c, shard, first):
        at = pl.ds(pl.multiple_of(shard * rows, rows), rows)
        part = pl.ds(pl.multiple_of(c * width, width), width)
        x = xbuf[c, at, :]
        add = jnp.dot(x, wkv[part, :], preferred_element_type=jnp.float32)
        if first:
            acc_kv[at, :] = add
        else:
            acc_kv[at, :] += add

        @pl.loop(0, query_width // tile_q)
        def _(k):
            columns = pl.ds(pl.multiple_of(k * tile_q, tile_q), tile_q)
            more = jnp.dot(
                xbuf[c, at, :], wq[part, columns], preferred_element_type=jnp.float32
            )
            if first:
                acc_q[at, columns] = more
            else:
                acc_q[at, columns] += more

    acc_q[...] = jnp.zeros_like(acc_q)
    acc_kv[...] = jnp.zeros_like(acc_kv)

    @pl.loop(0, chunks)
    def _(c):
        own_copy(c).wait()
        for copy in weight_copies(c):
            copy.wait()
        unit(c, t, False)

    for copy in own_adapters:
        copy.wait()

    share = chunks // n
    last_phase = jnp.maximum(t, n - 1 - t)
    low_at = share * (jnp.minimum(t, n - 1 - t) + 1) - 1

    def part_copy(d):
        to = lax.rem(t + d, n)
        return pltpu.make_async_remote_copy(
            src_ref=low_part.at[pl.ds(to * rows, rows), :],
            dst_ref=low_got.at[t],
            send_sem=part_send.at[d],
            recv_sem=part_recv.at[d],
            device_id={"tensor": to},
            device_id_type=MESH,
        )

    def part_arrival(d):
        source = lax.rem(t + n - d, n)
        return pltpu.make_async_remote_copy(
            src_ref=low_got.at[source],
            dst_ref=low_got.at[source],
            send_sem=part_send.at[d],
            recv_sem=part_recv.at[d],
            device_id={"tensor": source},
            device_id_type=MESH,
        )

    def low_copy(d):
        to = lax.rem(t + d, n)
        held = low_all.at[pl.ds(t * rows, rows), :]
        return pltpu.make_async_remote_copy(
            src_ref=held,
            dst_ref=held,
            send_sem=low_send.at[d],
            recv_sem=low_recv.at[d],
            device_id={"tensor": to},
            device_id_type=MESH,
        )

    def low_arrival(d):
        source = lax.rem(t + n - d, n)
        held = low_all.at[pl.ds(source * rows, rows), :]
        return pltpu.make_async_remote_copy(
            src_ref=held,
            dst_ref=held,
            send_sem=low_send.at[d],
            recv_sem=low_recv.at[d],
            device_id={"tensor": source},
            device_id_type=MESH,
        )

    def adapters_arrive():
        for d in range(1, stores):
            source = lax.rem(s + stores - d, stores)
            for i, (_, held) in enumerate(adapter_pairs):
                block = adapter_block(held, i, source)
                pltpu.make_async_remote_copy(
                    src_ref=block,
                    dst_ref=block,
                    send_sem=adapter_send.at[i, d],
                    recv_sem=adapter_recv.at[i, d],
                    device_id={"store": source},
                    device_id_type=MESH,
                ).wait_recv()

    def low_first():
        adapters_arrive()
        low_part[...] = jnp.zeros_like(low_part)
        for p in range(stores):
            picked = jnp.zeros(low_part.shape, jnp.float32)
            for k in range(share):
                picked += lax.dot_general(
                    xbuf[t * share + k],
                    down[p, :, k * width : (k + 1) * width],
                    (((1,), (1,)), ((), ())),
                    preferred_element_type=jnp.float32,
                )
            low_part[...] += picked * mask_ref[:, p : p + 1]
        for d in range(1, n):
            part_copy(d).start()

    def low_second():
        at = pl.ds(pl.multiple_of(t * rows, rows), rows)
        low_got[t] = low_part[at, :]
        for d in range(1, n):
            part_arrival(d).wait_recv()
        whole = low_got[0]
        for j in range(1, n):
            whole += low_got[j]
        low_all[at, :] = whole.astype(jnp.bfloat16)
        for d in range(1, n):
            low_copy(d).start()

    def low_third():
        for d in range(1, n):
            low_arrival(d).wait_recv()
        low = low_all[...].astype(jnp.float32)
        turned = pltpu.roll(low, ADAPTER_RANK, 1)
        in_lower = lax.broadcasted_iota(jnp.int32, low.shape, 1) < ADAPTER_RANK
        twice_q = jnp.where(in_lower, low, turned)
        twice_kv = jnp.where(in_lower, turned, low)
        masks = [
            jnp.where(in_lower, mask_ref[:, 2 * p : 2 * p + 1], mask_ref[:, 2 * p + 1 : 2 * p + 2])
            for p in range(stores // 2)
        ]
        spread_q = jnp.concatenate([(twice_q * m).astype(jnp.bfloat16) for m in masks], axis=1)
        spread_kv = jnp.concatenate([(twice_kv * m).astype(jnp.bfloat16) for m in masks], axis=1)
        acc_kv[...] += adapter_scale * jnp.dot(
            spread_kv, upkv[...], preferred_element_type=jnp.float32
        )
        for k in range(query_width // tile_q):
            columns = slice(k * tile_q, (k + 1) * tile_q)
            acc_q[:, columns] += adapter_scale * jnp.dot(
                spread_q, upq[:, columns], preferred_element_type=jnp.float32
            )

    depth = min(2, chunks)

    @pl.loop(0, (n - 1) * chunks)
    def _(step):
        p = step // chunks + 1
        i = step % chunks
        here = (t - p >= 0, t + p < n)
        for side in range(2):

            @pl.when(jnp.logical_and(here[side], can_send[side]))
            def _():
                back = step + chunks - depth
                arrival(side, p, i).wait_recv()
                stream_copy(side, back // chunks, back % chunks, False).wait_send()
                stream_copy(side, p, i, False).start()

            @pl.when(jnp.logical_and(here[side], jnp.logical_not(can_send[side])))
            def _():
                arrival(side, p, i).wait_recv()

        for side in range(2):

            @pl.when(here[side])
            def _():
                unit(place(side, i), t - p if side == 0 else t + p, False)

        @pl.when(jnp.logical_and(p == last_phase, i == low_at))
        def _():
            low_first()

        @pl.when(jnp.logical_and(p == last_phase, i == low_at + 2))
        def _():
            low_second()

        @pl.when(jnp.logical_and(p == last_phase, i == chunks - 2))
        def _():
            low_third()

    def rotated(value, cosine, sine):
        return value * cosine + pltpu.roll(value, HEAD_SIZE // 2, 1) * sine

    for m in range(pair_heads):
        value = acc_kv[:, m * HEAD_SIZE : (m + 1) * HEAD_SIZE]
        kv_heads[m] = rotated(value, kcos_ref[...], ksin_ref[...]).astype(jnp.bfloat16)
    partner = t + 1 - 2 * (t % 2)
    kv_copy = pltpu.make_async_remote_copy(
        src_ref=kv_heads.at[pl.ds(kv_first(partner), kv_used)],
        dst_ref=kv_got,
        send_sem=kv_sem.at[0],
        recv_sem=kv_sem.at[1],
        device_id={"tensor": partner},
        device_id_type=MESH,
    )
    kv_copy.start()
    for h in range(head_local):
        columns = slice(h * HEAD_SIZE, (h + 1) * HEAD_SIZE)
        query_out[:, columns] = rotated(acc_q[:, columns], cos_ref[...], sin_ref[...]).astype(
            jnp.bfloat16
        )
    own_out[...] = kv_heads[pl.ds(kv_first(t), kv_used)]
    for copy in adapter_sends:
        copy.wait_send()
    for d in range(1, n):
        part_copy(d).wait_send()
        low_copy(d).wait_send()

    @pl.loop(0, chunks - depth)
    def _(k):
        for side in range(2):

            @pl.when(can_send[side])
            def _():
                stream_copy(side, 0, k, False).wait_send()

    @pl.loop(0, depth)
    def _(k):
        for side in range(2):

            @pl.when(can_send[side])
            def _():
                reach = t if side == 0 else n - 1 - t
                back = (reach + 1) * chunks - depth + k
                stream_copy(side, back // chunks, back % chunks, False).wait_send()

    kv_copy.wait()
    other_out[...] = kv_got[...]


def attend_kernel(query_ref, keys_ref, values_ref, row_ref, column_ref, out_ref, bias_ref):
    count = query_ref.shape[0]
    block = 128
    scale = 1.0 / math.sqrt(HEAD_SIZE)

    @pl.when(pl.program_id(0) == 0)
    def _():
        place_row = lax.broadcasted_iota(jnp.int32, (count, count), 0)
        place_column = lax.broadcasted_iota(jnp.int32, (count, count), 1)
        allowed = jnp.logical_and(
            column_ref[...] == row_ref[...], place_row >= place_column
        )
        bias_ref[...] = jnp.where(allowed, 0.0, -1e30)

    for b in range(count // block):
        low = max(0, (b + 1) * block - block - MAX_RUN)
        high = (b + 1) * block
        at = slice(b * block, high)
        scores = lax.dot_general(
            query_ref[at, :],
            keys_ref[0, low:high, :],
            (((1,), (1,)), ((), ())),
            preferred_element_type=jnp.float32,
        )
        scores = scores * scale + bias_ref[at, low:high]
        scores = jnp.exp(scores - jnp.max(scores, axis=1, keepdims=True))
        weights = (scores * (1.0 / jnp.sum(scores, axis=1, keepdims=True))).astype(jnp.bfloat16)
        out_ref[at, :] = jnp.dot(
            weights, values_ref[0, low:high, :], preferred_element_type=jnp.float32
        ).astype(jnp.bfloat16)


def attend(query, keys, values, segment_row):
    count, query_width = query.shape
    head_local = query_width // HEAD_SIZE
    per_kv = head_local // keys.shape[0]
    kv_spec = pl.BlockSpec((1, count, HEAD_SIZE), lambda h: (h // per_kv, 0, 0))
    return pl.pallas_call(
        attend_kernel,
        grid=(head_local,),
        in_specs=[
            pl.BlockSpec((count, HEAD_SIZE), lambda h: (0, h)),
            kv_spec,
            kv_spec,
            pl.BlockSpec((1, count), lambda h: (0, 0)),
            pl.BlockSpec((count, 1), lambda h: (0, 0)),
        ],
        out_specs=pl.BlockSpec((count, HEAD_SIZE), lambda h: (0, h)),
        out_shape=jax.ShapeDtypeStruct((count, query_width), jnp.bfloat16),
        scratch_shapes=[pltpu.VMEM((count, count), jnp.float32)],
        name="attend",
    )(query, keys, values, segment_row[None, :], segment_row[:, None])


def on_device(
    tokens,
    query_weight,
    key_value_weight,
    adapter_down_maps,
    adapter_up_query,
    adapter_up_key_value,
    adapter_row_table,
    request_adapter_ids,
    token_request_ids,
):
    tensor_rank = lax.axis_index("tensor")
    store_rank = lax.axis_index("store")
    n = lax.axis_size("tensor")
    stores = lax.axis_size("store")
    position_count = adapter_down_maps.shape[0]
    adapter_total = adapter_row_table.shape[0]
    lookup = (
        request_adapter_ids[:, :, None] == jnp.arange(adapter_total, dtype=jnp.int32)[None, None, :]
    ).astype(jnp.int32)
    slot_table = jnp.sum(lookup * adapter_row_table[None, None, :], axis=2)
    my_slots = lax.dynamic_index_in_dim(slot_table, store_rank, 0, keepdims=False)
    mine = slot_table // position_count == store_rank
    index = jnp.sum(jnp.where(mine, slot_table % position_count, 0), axis=1)
    down, up_query, up_keyval = select_adapters(
        index, (adapter_down_maps, adapter_up_query, adapter_up_key_value)
    )
    segment_row = token_request_ids[0]
    members = segment_row[:, None] == jnp.arange(STORE_REQUESTS, dtype=jnp.int32)[None, :]
    holder = jnp.sum(jnp.where(members, (my_slots // position_count)[None, :], 0), axis=1)
    mask = (holder[:, None] == jnp.arange(stores, dtype=jnp.int32)[None, :]).astype(jnp.float32)
    cosine, sine = rotary_tables(token_positions(segment_row))
    holds_keys = tensor_rank % 2 == 0
    key_cosine = jnp.where(holds_keys, cosine, 1.0)
    key_sine = jnp.where(holds_keys, sine, 0.0)

    rows, model_width = tokens.shape
    total = rows * n
    query_width = query_weight.shape[1]
    keyval_width = key_value_weight.shape[1]
    chunks = max(8, n)
    width = model_width // chunks
    pair_heads = keyval_width // HEAD_SIZE
    kv_used = max(query_width // HEAD_SIZE // (QUERY_HEADS // KEY_VALUE_HEADS), 1)
    two_ranks = 2 * ADAPTER_RANK
    hbm = pl.BlockSpec(memory_space=pl.ANY)
    vmem = pl.BlockSpec(memory_space=pltpu.VMEM)
    dma = pltpu.SemaphoreType.DMA
    query, own, other = pl.pallas_call(
        functools.partial(project_kernel, n, stores, chunks),
        in_specs=[hbm] * 6 + [vmem] * 5,
        out_specs=[vmem] * 3,
        out_shape=[
            jax.ShapeDtypeStruct((total, query_width), jnp.bfloat16),
            jax.ShapeDtypeStruct((kv_used, total, HEAD_SIZE), jnp.bfloat16),
            jax.ShapeDtypeStruct((kv_used, total, HEAD_SIZE), jnp.bfloat16),
        ],
        scratch_shapes=[
            pltpu.VMEM((chunks, total, width), jnp.bfloat16),
            pltpu.VMEM((model_width, query_width), jnp.bfloat16),
            pltpu.VMEM((model_width, keyval_width), jnp.bfloat16),
            pltpu.VMEM((total, query_width), jnp.float32),
            pltpu.VMEM((total, keyval_width), jnp.float32),
            pltpu.VMEM((stores, two_ranks, model_width // n), jnp.bfloat16),
            pltpu.VMEM((stores * ADAPTER_RANK, query_width), jnp.bfloat16),
            pltpu.VMEM((stores * ADAPTER_RANK, keyval_width), jnp.bfloat16),
            pltpu.VMEM((total, two_ranks), jnp.float32),
            pltpu.VMEM((n, rows, two_ranks), jnp.float32),
            pltpu.VMEM((total, two_ranks), jnp.bfloat16),
            pltpu.VMEM((pair_heads, total, HEAD_SIZE), jnp.bfloat16),
            pltpu.VMEM((kv_used, total, HEAD_SIZE), jnp.bfloat16),
            dma((chunks,)),
            dma((2, chunks)),
            dma((2, n, chunks)),
            dma((2, n, chunks)),
            dma((3, stores)),
            dma((3, stores)),
            dma((3,)),
            dma((n,)),
            dma((n,)),
            dma((n,)),
            dma((n,)),
            dma((2,)),
        ],
        compiler_params=pltpu.CompilerParams(
            collective_id=0, has_side_effects=True, vmem_limit_bytes=67043328
        ),
        name="project",
    )(
        tokens,
        query_weight,
        key_value_weight,
        down,
        up_query,
        up_keyval,
        mask,
        cosine,
        sine,
        key_cosine,
        key_sine,
    )
    keys = jnp.where(holds_keys, own, other)
    values = jnp.where(holds_keys, other, own)
    return attend(query, keys, values, segment_row)


def solution(mesh):
    return jax.shard_map(
        on_device,
        mesh=mesh,
        in_specs=(
            P(("groups", "store", "tensor"), None),
            P(None, "tensor"),
            P(None, "tensor"),
            P("store", None, "tensor"),
            P("store", None, "tensor"),
            P("store", None, "tensor"),
            P("groups"),
            P("groups", None),
            P(("groups", "store"), None),
        ),
        out_specs=P(("groups", "store"), "tensor"),
        check_vma=False,
    )
```

time: 271 us -> 200 us (0.74)
  Pallas kernels: 0 us -> 190 us
  waiting for transfers between devices: 119 us -> 0 us
  matrix products: 71 us -> 0 us
  blocking collectives: 21.4 us -> 0 us
  other arithmetic: 22.4 us -> 8.24 us
  between operations: 13.7 us -> 0.04 us
  starting transfers between devices: 11.6 us -> 0 us
  local copies, waits for them, and re-layouts: 10.9 us -> 1.53 us
    pallas_call x0 -> x3, Pallas kernels: none -> 190 us  [the longest x1 159 us: on_device(): pl.pallas_call(functools.partial(project_kernel, n, stores, chunks), in_s...]
    all_gather x1 -> x0, waiting for transfers between devices: 89.3 us -> none  [on_device(): rows_piece = lax.all_gather(tokens, 'tensor', axis=0, tiled=True)]
    dot_general x13 -> x0, matrix products: 71 us -> none  [the longest x1 23.8 us: on_device(): jnp.dot(rows_piece, query_weight, preferred_element_type=jnp.float32)]
    all_to_all x3 -> x0, waiting for transfers between devices: 29.5 us -> none  [the longest x1 20.5 us: on_device(): lax.all_to_all(out_down, 'store', split_axis=0, concat_axis=0, tiled=True)]
    psum x1 -> x0, blocking collectives: 21.4 us -> none  [on_device(): lax.psum(joined[:, query_width + keyval_width:], 'tensor')]
    sub x2 -> x0, other arithmetic: 17.7 us -> none  [the longest x1 17.2 us: on_device(): scores = scores - jnp.max(scores, axis=-1, keepdims=True)]
    all_to_all x3 -> x0, starting transfers between devices: 11.6 us -> none  [the longest x1 4.24 us: on_device(): lax.all_to_all(out_keyval, 'store', split_axis=0, concat_axis=0, tiled=True)]
    convert_element_type x4 -> x0, local copies, waits for them, and re-layouts: 7.25 us -> none  [the longest x1 2.47 us: on_device(): out_down = select_rows(serving, adapter_down_maps).astype(jnp.bfloat16)]
  transfers between devices with their start and end apart: 5 -> 0, of which waited for: 4 -> 0; matrix products, arithmetic and copies ran while one was open for 19% -> 0% of each run, Pallas kernels for 0% -> 0%
where the time goes in v1:
time: 200 us
  Pallas kernels  190 us (95%)
  other arithmetic  8.24 us (4%)
    pallas_call x1, Pallas kernels, on_device(): pl.pallas_call(functools.partial(project_kernel, n, stores, chunks), in_s...  159 us
    pallas_call x1, Pallas kernels, attend(): pl.pallas_call(attend_kernel, grid=(head_local,), in_specs=[pl.BlockSpec(...  26.2 us
    pallas_call x1, Pallas kernels, select_adapters(): pl.pallas_call(select_kernel, grid_spec=pltpu.PrefetchScalarGridSpec(num_...  4.88 us

profile of v1, /device:TPU:0, one launch (start us, length us, event | category | flops | bytes accessed | tf_op | source)
XLA Modules:
  0.0 199.8 jit_solution(1472653229743235614)
XLA Ops:
  0.0 0.9 select_reduce_fusion.2
  0.9 0.8 convert_reduce_fusion
  1.7 0.2 reduce-window.8
  1.9 0.8 select_reduce_fusion
  2.7 1.0 fusion.1
  3.7 1.2 broadcast_select_fusion.2
  4.9 0.9 fusion.mask_ref
  5.8 0.6 fusion.4.index_ref
  6.4 4.9 %select_adapters.1 = (bf16[4,128,2048]{2,1,0:T(8,128)(2,1)}, bf16[4,64,2048]{2,1,0:T(8,128)(2,1)}, bf16[4,64,512]{2,1,0:T(8,128)(2,1)}) custom-call(s32[4]{0:T(128)} %fusion.4.index_ref, bf16[8,128,2048]{2,1,0:T(8,128)(2,1)} %down_ref.1, bf16[8,64,2048]{2,1,0:T(8,128)(2,1)} %query_ref.1, bf16[8,64,512]{2,1,0:T(8,128)(2,1)} %keyval_ref.1), custom_call_target="tpu_custom_call" | custom-call | tf_op jit(solution)/shard_map/select_adapters/pallas_call | solution.py:63
  11.3 159.0 %project.1 = (bf16[512,2048]{1,0:T(8,128)(2,1)}, bf16[2,512,128]{2,1,0:T(8,128)(2,1)}, bf16[2,512,128]{2,1,0:T(8,128)(2,1)}) custom-call(bf16[128,8192]{1,0:T(8,128)(2,1)} %tokens_ref.1, bf16[8192,2048]{1,0:T(8,128)(2,1)} %wq_hbm.1, bf16[8192,512]{1,0:T(8,128)(2,1)} %wkv_hbm.1, bf16[4,128,2048]{2,1,0:T(8,128)(2,1)} %get-tuple-element.11.down_hbm, ...), custom_call_target="tpu_custom_call" | custom-call | tf_op jit(solution)/shard_map/project/pallas_call | solution.py:576
  170.3 1.9 broadcast_select_fusion
  172.1 1.5 copy.11.column_ref
  173.7 26.2 %attend.1 = bf16[512,2048]{1,0:T(8,128)(2,1)} custom-call(bf16[512,2048]{1,0:T(8,128)(2,1)} %get-tuple-element.14.query_ref, bf16[2,512,128]{2,1,0:T(8,128)(2,1)} %get-tuple-element.22.keys_ref, bf16[2,512,128]{2,1,0:T(8,128)(2,1)} %get-tuple-element.21.values_ref, s32[1,512]{1,0:T(1,128)} %row_ref.1, s32[512,1]{1,0:T(8,128)} %copy.11.column_ref), custom_call_target="tpu_custom_call" | custom-call | tf_op jit(solution)/shard_map/attend/pallas_call | solution.py:511
  (4 shorter events, 0.0 us)

commit v2 on v1

--- a/solution.py
+++ b/solution.py
@@ -21,29 +21,8 @@
 rope_theta = 500000.0
 
 
-def token_positions(segment_row):
-    members = segment_row[:, None] == jnp.arange(STORE_REQUESTS, dtype=jnp.int32)[None, :]
-    counts = jnp.sum(members.astype(jnp.int32), axis=0)
-    starts = jnp.cumsum(counts) - counts
-    first_index = jnp.sum(jnp.where(members, starts[None, :], 0), axis=1)
-    return jnp.arange(segment_row.shape[0], dtype=jnp.int32) - first_index
-
-
 MAX_RUN = 256
 MESH = pl.DeviceIdType.MESH
-
-
-def rotary_tables(positions):
-    half_size = HEAD_SIZE // 2
-    exponent = jnp.arange(half_size, dtype=jnp.float32) * (2.0 / HEAD_SIZE)
-    frequency = jnp.exp(-exponent * math.log(rope_theta))
-    angles = positions.astype(jnp.float32)[:, None] * frequency[None, :]
-    cosine = jnp.cos(angles)
-    sine = jnp.sin(angles)
-    return (
-        jnp.concatenate([cosine, cosine], axis=1),
-        jnp.concatenate([-sine, sine], axis=1),
-    )
 
 
 def select_kernel(index_ref, down_ref, query_ref, keyval_ref, down_out, query_out, keyval_out):
@@ -80,20 +59,17 @@
     n,
     stores,
     chunks,
+    position_count,
     tokens_ref,
     wq_hbm,
     wkv_hbm,
     down_hbm,
     upq_hbm,
     upkv_hbm,
-    mask_ref,
-    cos_ref,
-    sin_ref,
-    kcos_ref,
-    ksin_ref,
-    query_out,
-    own_out,
-    other_out,
+    slot_ref,
+    segment_ref,
+    frequency_ref,
+    out_ref,
     xbuf,
     wq,
     wkv,
@@ -107,6 +83,12 @@
     low_all,
     kv_heads,
     kv_got,
+    keys_ref,
+    values_ref,
+    bias_ref,
+    cos_ref,
+    sin_ref,
+    holder_ref,
     token_sem,
     weight_sem,
     recv_sem,
@@ -119,6 +101,7 @@
     low_send,
     low_recv,
     kv_sem,
+    out_sem,
 ):
     t = lax.axis_index("tensor")
     s = lax.axis_index("store")
@@ -257,6 +240,29 @@
 
     acc_q[...] = jnp.zeros_like(acc_q)
     acc_kv[...] = jnp.zeros_like(acc_kv)
+    holds_keys = t % 2 == 0
+
+    place_row = lax.broadcasted_iota(jnp.int32, (total, total), 0)
+    place_column = lax.broadcasted_iota(jnp.int32, (total, total), 1)
+    across = segment_ref[...].astype(jnp.float32)
+    down_column = jnp.sum(jnp.where(place_row == place_column, across, 0.0), axis=1, keepdims=True)
+    allowed = jnp.logical_and(down_column == across, place_row >= place_column)
+    bias_ref[...] = jnp.where(allowed, 0.0, -1e30)
+    first_index = jnp.sum(jnp.where(across < down_column, 1.0, 0.0), axis=1, keepdims=True)
+    place_token = lax.broadcasted_iota(jnp.int32, (total, 1), 0).astype(jnp.float32)
+    angles = (place_token - first_index) * frequency_ref[...]
+    lane = lax.broadcasted_iota(jnp.int32, angles.shape, 1)
+    sine = jnp.sin(angles)
+    cos_ref[...] = jnp.cos(angles)
+    sin_ref[...] = jnp.where(lane < HEAD_SIZE // 2, -sine, sine)
+    holder = jnp.zeros((total, 1), jnp.float32)
+    for k in range(STORE_REQUESTS):
+        owner = lax.div(slot_ref[s, k], position_count).astype(jnp.float32)
+        holder += jnp.where(down_column == float(k), owner, 0.0)
+    holder_ref[...] = holder
+
+    def mask_of(p):
+        return jnp.where(holder_ref[...] == float(p), 1.0, 0.0)
 
     @pl.loop(0, chunks)
     def _(c):
@@ -344,7 +350,7 @@
                     (((1,), (1,)), ((), ())),
                     preferred_element_type=jnp.float32,
                 )
-            low_part[...] += picked * mask_ref[:, p : p + 1]
+            low_part[...] += picked * mask_of(p)
         for d in range(1, n):
             part_copy(d).start()
 
@@ -369,7 +375,7 @@
         twice_q = jnp.where(in_lower, low, turned)
         twice_kv = jnp.where(in_lower, turned, low)
         masks = [
-            jnp.where(in_lower, mask_ref[:, 2 * p : 2 * p + 1], mask_ref[:, 2 * p + 1 : 2 * p + 2])
+            jnp.where(in_lower, mask_of(2 * p), mask_of(2 * p + 1))
             for p in range(stores // 2)
         ]
         spread_q = jnp.concatenate([(twice_q * m).astype(jnp.bfloat16) for m in masks], axis=1)
@@ -383,7 +389,34 @@
                 spread_q, upq[:, columns], preferred_element_type=jnp.float32
             )
 
-    depth = min(2, chunks)
+    def rotated(value, cosine, sine):
+        return value * cosine + pltpu.roll(value, HEAD_SIZE // 2, 1) * sine
+
+    ends_first = t >= n - t
+    early_start = pl.multiple_of(jnp.where(ends_first, rows, 0), rows)
+    late_start = pl.multiple_of(jnp.where(ends_first, 0, total - rows), rows)
+    partner = t + 1 - 2 * (t % 2)
+
+    def finish_keyval(start, count):
+        at = pl.ds(start, count)
+        cosine = jnp.where(holds_keys, cos_ref[at, :], 1.0)
+        sine = jnp.where(holds_keys, sin_ref[at, :], 0.0)
+        for m in range(pair_heads):
+            value = acc_kv[at, m * HEAD_SIZE : (m + 1) * HEAD_SIZE]
+            kv_heads[m, at, :] = rotated(value, cosine, sine).astype(jnp.bfloat16)
+
+    def keyval_copy(start, count, which):
+        at = pl.ds(start, count)
+        return pltpu.make_async_remote_copy(
+            src_ref=kv_heads.at[pl.ds(kv_first(partner), kv_used), at, :],
+            dst_ref=kv_got.at[:, at, :],
+            send_sem=kv_sem.at[0, which],
+            recv_sem=kv_sem.at[1, which],
+            device_id={"tensor": partner},
+            device_id_type=MESH,
+        )
+
+    depth = min(4, chunks)
 
     @pl.loop(0, (n - 1) * chunks)
     def _(step):
@@ -413,36 +446,18 @@
         def _():
             low_first()
 
-        @pl.when(jnp.logical_and(p == last_phase, i == low_at + 2))
+        @pl.when(jnp.logical_and(p == last_phase, i == low_at + 1))
         def _():
             low_second()
 
         @pl.when(jnp.logical_and(p == last_phase, i == chunks - 2))
         def _():
             low_third()
-
-    def rotated(value, cosine, sine):
-        return value * cosine + pltpu.roll(value, HEAD_SIZE // 2, 1) * sine
-
-    for m in range(pair_heads):
-        value = acc_kv[:, m * HEAD_SIZE : (m + 1) * HEAD_SIZE]
-        kv_heads[m] = rotated(value, kcos_ref[...], ksin_ref[...]).astype(jnp.bfloat16)
-    partner = t + 1 - 2 * (t % 2)
-    kv_copy = pltpu.make_async_remote_copy(
-        src_ref=kv_heads.at[pl.ds(kv_first(partner), kv_used)],
-        dst_ref=kv_got,
-        send_sem=kv_sem.at[0],
-        recv_sem=kv_sem.at[1],
-        device_id={"tensor": partner},
-        device_id_type=MESH,
-    )
-    kv_copy.start()
-    for h in range(head_local):
-        columns = slice(h * HEAD_SIZE, (h + 1) * HEAD_SIZE)
-        query_out[:, columns] = rotated(acc_q[:, columns], cos_ref[...], sin_ref[...]).astype(
-            jnp.bfloat16
-        )
-    own_out[...] = kv_heads[pl.ds(kv_first(t), kv_used)]
+            finish_keyval(early_start, total - rows)
+            keyval_copy(early_start, total - rows, 0).start()
+
+    finish_keyval(late_start, rows)
+    keyval_copy(late_start, rows, 1).start()
     for copy in adapter_sends:
         copy.wait_send()
     for d in range(1, n):
@@ -467,62 +482,80 @@
                 back = (reach + 1) * chunks - depth + k
                 stream_copy(side, back // chunks, back % chunks, False).wait_send()
 
-    kv_copy.wait()
-    other_out[...] = kv_got[...]
-
-
-def attend_kernel(query_ref, keys_ref, values_ref, row_ref, column_ref, out_ref, bias_ref):
-    count = query_ref.shape[0]
+    per_chunk = width // HEAD_SIZE
+    for h in range(head_local):
+        columns = slice(h * HEAD_SIZE, (h + 1) * HEAD_SIZE)
+        inside = h % per_chunk * HEAD_SIZE
+        xbuf[h // per_chunk, :, inside : inside + HEAD_SIZE] = rotated(
+            acc_q[:, columns], cos_ref[...], sin_ref[...]
+        ).astype(jnp.bfloat16)
+
+    keyval_copy(early_start, total - rows, 0).wait()
+    keyval_copy(late_start, rows, 1).wait()
+    own_first = kv_first(t)
+    for g in range(kv_used):
+        values_ref[g, :, HEAD_SIZE:] = jnp.ones((total, HEAD_SIZE), jnp.bfloat16)
+
+        @pl.when(holds_keys)
+        def _():
+            keys_ref[g] = kv_heads[own_first + g]
+            values_ref[g, :, :HEAD_SIZE] = kv_got[g]
+
+        @pl.when(jnp.logical_not(holds_keys))
+        def _():
+            keys_ref[g] = kv_got[g]
+            values_ref[g, :, :HEAD_SIZE] = kv_heads[own_first + g]
+
+    per_kv = head_local // kv_used
+    batch = 4
+    batches_per_chunk = per_chunk // batch
     block = 128
-    scale = 1.0 / math.sqrt(HEAD_SIZE)
-
-    @pl.when(pl.program_id(0) == 0)
-    def _():
-        place_row = lax.broadcasted_iota(jnp.int32, (count, count), 0)
-        place_column = lax.broadcasted_iota(jnp.int32, (count, count), 1)
-        allowed = jnp.logical_and(
-            column_ref[...] == row_ref[...], place_row >= place_column
-        )
-        bias_ref[...] = jnp.where(allowed, 0.0, -1e30)
-
-    for b in range(count // block):
-        low = max(0, (b + 1) * block - block - MAX_RUN)
-        high = (b + 1) * block
-        at = slice(b * block, high)
-        scores = lax.dot_general(
-            query_ref[at, :],
-            keys_ref[0, low:high, :],
-            (((1,), (1,)), ((), ())),
-            preferred_element_type=jnp.float32,
-        )
-        scores = scores * scale + bias_ref[at, low:high]
-        scores = jnp.exp(scores - jnp.max(scores, axis=1, keepdims=True))
-        weights = (scores * (1.0 / jnp.sum(scores, axis=1, keepdims=True))).astype(jnp.bfloat16)
-        out_ref[at, :] = jnp.dot(
-            weights, values_ref[0, low:high, :], preferred_element_type=jnp.float32
-        ).astype(jnp.bfloat16)
-
-
-def attend(query, keys, values, segment_row):
-    count, query_width = query.shape
-    head_local = query_width // HEAD_SIZE
-    per_kv = head_local // keys.shape[0]
-    kv_spec = pl.BlockSpec((1, count, HEAD_SIZE), lambda h: (h // per_kv, 0, 0))
-    return pl.pallas_call(
-        attend_kernel,
-        grid=(head_local,),
-        in_specs=[
-            pl.BlockSpec((count, HEAD_SIZE), lambda h: (0, h)),
-            kv_spec,
-            kv_spec,
-            pl.BlockSpec((1, count), lambda h: (0, 0)),
-            pl.BlockSpec((count, 1), lambda h: (0, 0)),
-        ],
-        out_specs=pl.BlockSpec((count, HEAD_SIZE), lambda h: (0, h)),
-        out_shape=jax.ShapeDtypeStruct((count, query_width), jnp.bfloat16),
-        scratch_shapes=[pltpu.VMEM((count, count), jnp.float32)],
-        name="attend",
-    )(query, keys, values, segment_row[None, :], segment_row[:, None])
+    scale = 1.0 / math.sqrt(HEAD_SIZE) / math.log(2.0)
+
+    def out_copy(q):
+        inside = pl.multiple_of(q % batches_per_chunk * batch * HEAD_SIZE, batch * HEAD_SIZE)
+        whole = pl.multiple_of(q * batch * HEAD_SIZE, batch * HEAD_SIZE)
+        return pltpu.make_async_copy(
+            xbuf.at[q // batches_per_chunk, :, pl.ds(inside, batch * HEAD_SIZE)],
+            out_ref.at[:, pl.ds(whole, batch * HEAD_SIZE)],
+            out_sem.at[q],
+        )
+
+    @pl.loop(0, head_local // batch)
+    def _(q):
+        chunk = q // batches_per_chunk
+        base = q % batches_per_chunk * batch
+        g = q * batch // per_kv
+        for pair in range(batch // 2):
+            lanes = [
+                pl.ds(pl.multiple_of((base + 2 * pair + k) * HEAD_SIZE, HEAD_SIZE), HEAD_SIZE)
+                for k in range(2)
+            ]
+            for b in range(total // block):
+                low = max(0, b * block - MAX_RUN)
+                high = (b + 1) * block
+                at = slice(b * block, high)
+                stacked = jnp.concatenate([xbuf[chunk, at, ln] for ln in lanes], axis=0)
+                scores = lax.dot_general(
+                    stacked,
+                    keys_ref[g, low:high, :],
+                    (((1,), (1,)), ((), ())),
+                    preferred_element_type=jnp.float32,
+                )
+                scores = scores.reshape(2, block, high - low) + bias_ref[at, low:high][None]
+                scores = (scores - jnp.max(scores, axis=2, keepdims=True)) * scale
+                weights = jnp.exp2(scores).astype(jnp.bfloat16).reshape(2 * block, high - low)
+                mixed = jnp.dot(
+                    weights, values_ref[g, low:high, :], preferred_element_type=jnp.float32
+                )
+                mixed = (mixed[:, :HEAD_SIZE] / mixed[:, HEAD_SIZE:]).astype(jnp.bfloat16)
+                for k in range(2):
+                    xbuf[chunk, at, lanes[k]] = mixed[k * block : (k + 1) * block]
+        out_copy(q).start()
+
+    @pl.loop(0, head_local // batch)
+    def _(q):
+        out_copy(q).wait()
 
 
 def on_device(
@@ -536,7 +569,6 @@
     request_adapter_ids,
     token_request_ids,
 ):
-    tensor_rank = lax.axis_index("tensor")
     store_rank = lax.axis_index("store")
     n = lax.axis_size("tensor")
     stores = lax.axis_size("store")
@@ -546,20 +578,15 @@
         request_adapter_ids[:, :, None] == jnp.arange(adapter_total, dtype=jnp.int32)[None, None, :]
     ).astype(jnp.int32)
     slot_table = jnp.sum(lookup * adapter_row_table[None, None, :], axis=2)
-    my_slots = lax.dynamic_index_in_dim(slot_table, store_rank, 0, keepdims=False)
     mine = slot_table // position_count == store_rank
     index = jnp.sum(jnp.where(mine, slot_table % position_count, 0), axis=1)
     down, up_query, up_keyval = select_adapters(
         index, (adapter_down_maps, adapter_up_query, adapter_up_key_value)
     )
-    segment_row = token_request_ids[0]
-    members = segment_row[:, None] == jnp.arange(STORE_REQUESTS, dtype=jnp.int32)[None, :]
-    holder = jnp.sum(jnp.where(members, (my_slots // position_count)[None, :], 0), axis=1)
-    mask = (holder[:, None] == jnp.arange(stores, dtype=jnp.int32)[None, :]).astype(jnp.float32)
-    cosine, sine = rotary_tables(token_positions(segment_row))
-    holds_keys = tensor_rank % 2 == 0
-    key_cosine = jnp.where(holds_keys, cosine, 1.0)
-    key_sine = jnp.where(holds_keys, sine, 0.0)
+    half_size = HEAD_SIZE // 2
+    exponent = jnp.arange(half_size, dtype=jnp.float32) * (2.0 / HEAD_SIZE)
+    frequency = jnp.exp(-exponent * math.log(rope_theta))
+    frequency = jnp.concatenate([frequency, frequency])[None, :]
 
     rows, model_width = tokens.shape
     total = rows * n
@@ -573,15 +600,11 @@
     hbm = pl.BlockSpec(memory_space=pl.ANY)
     vmem = pl.BlockSpec(memory_space=pltpu.VMEM)
     dma = pltpu.SemaphoreType.DMA
-    query, own, other = pl.pallas_call(
-        functools.partial(project_kernel, n, stores, chunks),
-        in_specs=[hbm] * 6 + [vmem] * 5,
-        out_specs=[vmem] * 3,
-        out_shape=[
-            jax.ShapeDtypeStruct((total, query_width), jnp.bfloat16),
-            jax.ShapeDtypeStruct((kv_used, total, HEAD_SIZE), jnp.bfloat16),
-            jax.ShapeDtypeStruct((kv_used, total, HEAD_SIZE), jnp.bfloat16),
-        ],
+    return pl.pallas_call(
+        functools.partial(project_kernel, n, stores, chunks, position_count),
+        in_specs=[hbm] * 6 + [pl.BlockSpec(memory_space=pltpu.SMEM), vmem, vmem],
+        out_specs=hbm,
+        out_shape=jax.ShapeDtypeStruct((total, query_width), jnp.bfloat16),
         scratch_shapes=[
             pltpu.VMEM((chunks, total, width), jnp.bfloat16),
             pltpu.VMEM((model_width, query_width), jnp.bfloat16),
@@ -596,6 +619,12 @@
             pltpu.VMEM((total, two_ranks), jnp.bfloat16),
             pltpu.VMEM((pair_heads, total, HEAD_SIZE), jnp.bfloat16),
             pltpu.VMEM((kv_used, total, HEAD_SIZE), jnp.bfloat16),
+            pltpu.VMEM((kv_used, total, HEAD_SIZE), jnp.bfloat16),
+            pltpu.VMEM((kv_used, total, 2 * HEAD_SIZE), jnp.bfloat16),
+            pltpu.VMEM((total, total), jnp.float32),
+            pltpu.VMEM((total, HEAD_SIZE), jnp.float32),
+            pltpu.VMEM((total, HEAD_SIZE), jnp.float32),
+            pltpu.VMEM((total, 1), jnp.float32),
             dma((chunks,)),
             dma((2, chunks)),
             dma((2, n, chunks)),
@@ -607,7 +636,8 @@
             dma((n,)),
             dma((n,)),
             dma((n,)),
-            dma((2,)),
+            dma((2, 2)),
+            dma((query_width // HEAD_SIZE // 4,)),
         ],
         compiler_params=pltpu.CompilerParams(
             collective_id=0, has_side_effects=True, vmem_limit_bytes=67043328
@@ -620,15 +650,10 @@
         down,
         up_query,
         up_keyval,
-        mask,
-        cosine,
-        sine,
-        key_cosine,
-        key_sine,
+        slot_table,
+        token_request_ids,
+        frequency,
     )
-    keys = jnp.where(holds_keys, own, other)
-    values = jnp.where(holds_keys, other, own)
-    return attend(query, keys, values, segment_row)
 
 
 def solution(mesh):

time: 200 us -> 185 us (0.925)
  Pallas kernels: 190 us -> 179 us
  other arithmetic: 8.24 us -> 2.3 us
  local copies, waits for them, and re-layouts: 1.53 us -> 3.75 us
    pallas_call x2 -> x1, Pallas kernels: 185 us -> 174 us  [on_device(): pl.pallas_call(functools.partial(project_kernel, n, stores, chunks, posit...]
    unnamed x0 -> x3, local copies, waits for them, and re-layouts: none -> 3.75 us
    select_n x2 -> x0, other arithmetic: 3.06 us -> none  [the longest x1 1.87 us: on_device(): values = jnp.where(holds_keys, other, own)]
where the time goes in v2:
time: 185 us
  Pallas kernels  179 us (97%)
  local copies, waits for them, and re-layouts  3.75 us (2%)
  other arithmetic  2.3 us (1%)
    pallas_call x1, Pallas kernels, on_device(): pl.pallas_call(functools.partial(project_kernel, n, stores, chunks, posit...  174 us
    pallas_call x1, Pallas kernels, select_adapters(): pl.pallas_call(select_kernel, grid_spec=pltpu.PrefetchScalarGridSpec(num_...  4.88 us
    unnamed x3, local copies, waits for them, and re-layouts  3.75 us

profile of v2, /device:TPU:0, one launch (start us, length us, event | category | flops | bytes accessed | tf_op | source)
XLA Modules:
  0.0 184.8 jit_solution(4600980206222058455)
XLA Ops:
  0.0 0.7 maximum_bitcast_fusion.frequency_ref
  0.7 0.9 select_reduce_fusion.slot_ref
  1.6 0.0 copy-start
  1.6 0.6 copy-done
  2.2 0.7 fusion.2.index_ref
  2.9 4.9 %select_adapters.1 = (bf16[4,128,2048]{2,1,0:T(8,128)(2,1)}, bf16[4,64,2048]{2,1,0:T(8,128)(2,1)}, bf16[4,64,512]{2,1,0:T(8,128)(2,1)}) custom-call(s32[4]{0:T(128)} %fusion.2.index_ref, bf16[8,128,2048]{2,1,0:T(8,128)(2,1)} %down_ref.1, bf16[8,64,2048]{2,1,0:T(8,128)(2,1)} %query_ref.1, bf16[8,64,512]{2,1,0:T(8,128)(2,1)} %keyval_ref.1), custom_call_target="tpu_custom_call" | custom-call | tf_op jit(solution)/shard_map/select_adapters/pallas_call | solution.py:42
  7.8 173.9 %project.1 = bf16[512,2048]{1,0:T(8,128)(2,1)} custom-call(bf16[128,8192]{1,0:T(8,128)(2,1)} %tokens_ref.1, bf16[8192,2048]{1,0:T(8,128)(2,1)} %wq_hbm.1, bf16[8192,512]{1,0:T(8,128)(2,1)} %wkv_hbm.1, bf16[4,128,2048]{2,1,0:T(8,128)(2,1)} %get-tuple-element.8.down_hbm, bf16[4,64,2048]{2,1,0:T(8,128)(2,1)} %get-tuple-element.9.upq_hbm, ...), custom_call_target="tpu_custom_call" | custom-call | tf_op jit(solution)/shard_map/project/pallas_call | solution.py:603
  181.7 3.2 %copy.11 = bf16[512,2048]{1,0:T(8,128)(2,1)} copy(bf16[512,2048]{1,0:T(8,128)(2,1)} %project.1) | data formatting | bytes 4194304
  (1 shorter events, 0.0 us)
Async XLA Ops:
  1.6 0.6 copy-start

commit v3 on v2

--- a/solution.py
+++ b/solution.py
@@ -25,34 +25,48 @@
 MESH = pl.DeviceIdType.MESH
 
 
-def select_kernel(index_ref, down_ref, query_ref, keyval_ref, down_out, query_out, keyval_out):
-    down_out[...] = down_ref[...]
-    query_out[...] = query_ref[...]
-    keyval_out[...] = keyval_ref[...]
-
-
-def select_adapters(index, stacks):
-    specs_in = [
-        pl.BlockSpec((1,) + stack.shape[1:], lambda i, index_ref: (index_ref[i], 0, 0))
-        for stack in stacks
-    ]
-    specs_out = [
-        pl.BlockSpec((1,) + stack.shape[1:], lambda i, index_ref: (i, 0, 0)) for stack in stacks
-    ]
+def select_kernel(
+    position_count, table_ref, request_ref, down_hbm, query_hbm, keyval_hbm, *rest
+):
+    outs, held, in_sem, out_sem = rest[:3], rest[3:6], rest[6], rest[7]
+    s = lax.axis_index("store")
+    stacks = (down_hbm, query_hbm, keyval_hbm)
+    loads = []
+    for i in range(request_ref.shape[0]):
+        index = 0
+        for k in range(STORE_REQUESTS):
+            slot = table_ref[request_ref[i, k]]
+            index += jnp.where(
+                lax.div(slot, position_count) == s, lax.rem(slot, position_count), 0
+            )
+        for j in range(3):
+            copy = pltpu.make_async_copy(stacks[j].at[index], held[j].at[i], in_sem.at[j, i])
+            copy.start()
+            loads.append((j, i, copy))
+    stores = []
+    for j, i, copy in loads:
+        copy.wait()
+        store = pltpu.make_async_copy(held[j].at[i], outs[j].at[i], out_sem.at[j, i])
+        store.start()
+        stores.append(store)
+    for store in stores:
+        store.wait()
+
+
+def select_adapters(table, requests, stacks):
+    hbm = pl.BlockSpec(memory_space=pl.ANY)
+    smem = pl.BlockSpec(memory_space=pltpu.SMEM)
+    count = requests.shape[0]
+    shapes = [(count,) + stack.shape[1:] for stack in stacks]
     return pl.pallas_call(
-        select_kernel,
-        grid_spec=pltpu.PrefetchScalarGridSpec(
-            num_scalar_prefetch=1,
-            grid=(index.shape[0],),
-            in_specs=specs_in,
-            out_specs=specs_out,
-        ),
-        out_shape=[
-            jax.ShapeDtypeStruct((index.shape[0],) + stack.shape[1:], stack.dtype)
-            for stack in stacks
-        ],
+        functools.partial(select_kernel, stacks[0].shape[0]),
+        in_specs=[smem, smem] + [hbm] * 3,
+        out_specs=[hbm] * 3,
+        out_shape=[jax.ShapeDtypeStruct(shape, jnp.bfloat16) for shape in shapes],
+        scratch_shapes=[pltpu.VMEM(shape, jnp.bfloat16) for shape in shapes]
+        + [pltpu.SemaphoreType.DMA((3, count)), pltpu.SemaphoreType.DMA((3, count))],
         name="select_adapters",
-    )(index, *stacks)
+    )(table, requests, *stacks)
 
 
 def project_kernel(
@@ -66,9 +80,9 @@
     down_hbm,
     upq_hbm,
     upkv_hbm,
-    slot_ref,
+    table_ref,
+    request_ref,
     segment_ref,
-    frequency_ref,
     out_ref,
     xbuf,
     wq,
@@ -79,6 +93,7 @@
     upq,
     upkv,
     low_part,
+    low_own,
     low_got,
     low_all,
     kv_heads,
@@ -250,14 +265,15 @@
     bias_ref[...] = jnp.where(allowed, 0.0, -1e30)
     first_index = jnp.sum(jnp.where(across < down_column, 1.0, 0.0), axis=1, keepdims=True)
     place_token = lax.broadcasted_iota(jnp.int32, (total, 1), 0).astype(jnp.float32)
-    angles = (place_token - first_index) * frequency_ref[...]
-    lane = lax.broadcasted_iota(jnp.int32, angles.shape, 1)
+    lane = lax.broadcasted_iota(jnp.int32, (total, HEAD_SIZE), 1)
+    exponent = lax.rem(lane, HEAD_SIZE // 2).astype(jnp.float32) * (2.0 / HEAD_SIZE)
+    angles = (place_token - first_index) * jnp.exp(-exponent * math.log(rope_theta))
     sine = jnp.sin(angles)
     cos_ref[...] = jnp.cos(angles)
     sin_ref[...] = jnp.where(lane < HEAD_SIZE // 2, -sine, sine)
     holder = jnp.zeros((total, 1), jnp.float32)
     for k in range(STORE_REQUESTS):
-        owner = lax.div(slot_ref[s, k], position_count).astype(jnp.float32)
+        owner = lax.div(table_ref[request_ref[s, k]], position_count).astype(jnp.float32)
         holder += jnp.where(down_column == float(k), owner, 0.0)
     holder_ref[...] = holder
 
@@ -340,7 +356,7 @@
 
     def low_first():
         adapters_arrive()
-        low_part[...] = jnp.zeros_like(low_part)
+        summed = jnp.zeros(low_part.shape, jnp.float32)
         for p in range(stores):
             picked = jnp.zeros(low_part.shape, jnp.float32)
             for k in range(share):
@@ -350,18 +366,18 @@
                     (((1,), (1,)), ((), ())),
                     preferred_element_type=jnp.float32,
                 )
-            low_part[...] += picked * mask_of(p)
+            summed += picked * mask_of(p)
+        low_part[...] = summed.astype(jnp.bfloat16)
+        low_own[...] = summed
         for d in range(1, n):
             part_copy(d).start()
 
     def low_second():
         at = pl.ds(pl.multiple_of(t * rows, rows), rows)
-        low_got[t] = low_part[at, :]
+        whole = low_own[at, :]
         for d in range(1, n):
             part_arrival(d).wait_recv()
-        whole = low_got[0]
-        for j in range(1, n):
-            whole += low_got[j]
+            whole += low_got[lax.rem(t + n - d, n)].astype(jnp.float32)
         low_all[at, :] = whole.astype(jnp.bfloat16)
         for d in range(1, n):
             low_copy(d).start()
@@ -507,16 +523,15 @@
             values_ref[g, :, :HEAD_SIZE] = kv_heads[own_first + g]
 
     per_kv = head_local // kv_used
-    batch = 4
+    batch = min(8, per_kv, per_chunk)
     batches_per_chunk = per_chunk // batch
     block = 128
     scale = 1.0 / math.sqrt(HEAD_SIZE) / math.log(2.0)
 
     def out_copy(q):
-        inside = pl.multiple_of(q % batches_per_chunk * batch * HEAD_SIZE, batch * HEAD_SIZE)
         whole = pl.multiple_of(q * batch * HEAD_SIZE, batch * HEAD_SIZE)
         return pltpu.make_async_copy(
-            xbuf.at[q // batches_per_chunk, :, pl.ds(inside, batch * HEAD_SIZE)],
+            wq.at[pl.ds(0, total), pl.ds(whole, batch * HEAD_SIZE)],
             out_ref.at[:, pl.ds(whole, batch * HEAD_SIZE)],
             out_sem.at[q],
         )
@@ -529,6 +544,12 @@
         for pair in range(batch // 2):
             lanes = [
                 pl.ds(pl.multiple_of((base + 2 * pair + k) * HEAD_SIZE, HEAD_SIZE), HEAD_SIZE)
+                for k in range(2)
+            ]
+            out_lanes = [
+                pl.ds(
+                    pl.multiple_of((q * batch + 2 * pair + k) * HEAD_SIZE, HEAD_SIZE), HEAD_SIZE
+                )
                 for k in range(2)
             ]
             for b in range(total // block):
@@ -550,7 +571,7 @@
                 )
                 mixed = (mixed[:, :HEAD_SIZE] / mixed[:, HEAD_SIZE:]).astype(jnp.bfloat16)
                 for k in range(2):
-                    xbuf[chunk, at, lanes[k]] = mixed[k * block : (k + 1) * block]
+                    wq[at, out_lanes[k]] = mixed[k * block : (k + 1) * block]
         out_copy(q).start()
 
     @pl.loop(0, head_local // batch)
@@ -569,25 +590,14 @@
     request_adapter_ids,
     token_request_ids,
 ):
-    store_rank = lax.axis_index("store")
     n = lax.axis_size("tensor")
     stores = lax.axis_size("store")
     position_count = adapter_down_maps.shape[0]
-    adapter_total = adapter_row_table.shape[0]
-    lookup = (
-        request_adapter_ids[:, :, None] == jnp.arange(adapter_total, dtype=jnp.int32)[None, None, :]
-    ).astype(jnp.int32)
-    slot_table = jnp.sum(lookup * adapter_row_table[None, None, :], axis=2)
-    mine = slot_table // position_count == store_rank
-    index = jnp.sum(jnp.where(mine, slot_table % position_count, 0), axis=1)
     down, up_query, up_keyval = select_adapters(
-        index, (adapter_down_maps, adapter_up_query, adapter_up_key_value)
+        adapter_row_table,
+        request_adapter_ids,
+        (adapter_down_maps, adapter_up_query, adapter_up_key_value),
     )
-    half_size = HEAD_SIZE // 2
-    exponent = jnp.arange(half_size, dtype=jnp.float32) * (2.0 / HEAD_SIZE)
-    frequency = jnp.exp(-exponent * math.log(rope_theta))
-    frequency = jnp.concatenate([frequency, frequency])[None, :]
-
     rows, model_width = tokens.shape
     total = rows * n
     query_width = query_weight.shape[1]
@@ -599,10 +609,11 @@
     two_ranks = 2 * ADAPTER_RANK
     hbm = pl.BlockSpec(memory_space=pl.ANY)
     vmem = pl.BlockSpec(memory_space=pltpu.VMEM)
+    smem = pl.BlockSpec(memory_space=pltpu.SMEM)
     dma = pltpu.SemaphoreType.DMA
     return pl.pallas_call(
         functools.partial(project_kernel, n, stores, chunks, position_count),
-        in_specs=[hbm] * 6 + [pl.BlockSpec(memory_space=pltpu.SMEM), vmem, vmem],
+        in_specs=[hbm] * 6 + [smem, smem, vmem],
         out_specs=hbm,
         out_shape=jax.ShapeDtypeStruct((total, query_width), jnp.bfloat16),
         scratch_shapes=[
@@ -614,8 +625,9 @@
             pltpu.VMEM((stores, two_ranks, model_width // n), jnp.bfloat16),
             pltpu.VMEM((stores * ADAPTER_RANK, query_width), jnp.bfloat16),
             pltpu.VMEM((stores * ADAPTER_RANK, keyval_width), jnp.bfloat16),
+            pltpu.VMEM((total, two_ranks), jnp.bfloat16),
             pltpu.VMEM((total, two_ranks), jnp.float32),
-            pltpu.VMEM((n, rows, two_ranks), jnp.float32),
+            pltpu.VMEM((n, rows, two_ranks), jnp.bfloat16),
             pltpu.VMEM((total, two_ranks), jnp.bfloat16),
             pltpu.VMEM((pair_heads, total, HEAD_SIZE), jnp.bfloat16),
             pltpu.VMEM((kv_used, total, HEAD_SIZE), jnp.bfloat16),
@@ -650,9 +662,9 @@
         down,
         up_query,
         up_keyval,
-        slot_table,
+        adapter_row_table,
+        request_adapter_ids,
         token_request_ids,
-        frequency,
     )
 
 

time: 185 us -> 172 us (0.930)
  Pallas kernels: 179 us -> 169 us
  other arithmetic: 2.3 us -> 0 us
    pallas_call x1, Pallas kernels: 174 us -> 165 us  [on_device(): pl.pallas_call(functools.partial(project_kernel, n, stores, chunks, posit...]
    unnamed x3 -> x1, local copies, waits for them, and re-layouts: 3.75 us -> 3.16 us
where the time goes in v3:
time: 172 us; the launch traced here: 173 us
  Pallas kernels  169 us (98%)
  local copies, waits for them, and re-layouts  3.16 us (2%)
    pallas_call x1, Pallas kernels, on_device(): pl.pallas_call(functools.partial(project_kernel, n, stores, chunks, posit...  165 us
    pallas_call x1, Pallas kernels, select_adapters(): pl.pallas_call(functools.partial(select_kernel, stacks[0].shape[0]), in_s...  4.46 us

profile of v3, /device:TPU:0, one launch (start us, length us, event | category | flops | bytes accessed | tf_op | source)
XLA Modules:
  0.0 172.5 jit_solution(883545038286717330)
XLA Ops:
  0.0 4.5 %select_adapters.1 = (bf16[4,128,2048]{2,1,0:T(8,128)(2,1)}, bf16[4,64,2048]{2,1,0:T(8,128)(2,1)}, bf16[4,64,512]{2,1,0:T(8,128)(2,1)}) custom-call(s32[32]{0:T(128)} %table_ref.3, s32[4,4]{1,0:T(4,128)} %request_ref.3, bf16[8,128,2048]{2,1,0:T(8,128)(2,1)} %down_hbm.1, bf16[8,64,2048]{2,1,0:T(8,128)(2,1)} %query_hbm.1, bf16[8,64,512]{2,1,0:T(8,128)(2,1)} %keyval_hbm.1), custom_call_target="tpu_custom_call" | custom-call | tf_op jit(solution)/shard_map/select_adapters/pallas_call | solution.py:61
  4.5 164.9 %project.1 = bf16[512,2048]{1,0:T(8,128)(2,1)} custom-call(bf16[128,8192]{1,0:T(8,128)(2,1)} %tokens_ref.1, bf16[8192,2048]{1,0:T(8,128)(2,1)} %wq_hbm.1, bf16[8192,512]{1,0:T(8,128)(2,1)} %wkv_hbm.1, bf16[4,128,2048]{2,1,0:T(8,128)(2,1)} %get-tuple-element.8.down_hbm, bf16[4,64,2048]{2,1,0:T(8,128)(2,1)} %get-tuple-element.9.upq_hbm, ...), custom_call_target="tpu_custom_call" | custom-call | tf_op jit(solution)/shard_map/project/pallas_call | solution.py:614
  169.4 3.2 %copy.11 = bf16[512,2048]{1,0:T(8,128)(2,1)} copy(bf16[512,2048]{1,0:T(8,128)(2,1)} %project.1) | data formatting | bytes 4194304
